TPU v7x, 256 devices: a whole 4x4x8 slice. The times are simulated.
256 devices in a mesh: section: 32 (over z_lo, y, x), tp: 8 (over z_hi, core).
Axes of the slice: x: 4, y: 4, z: 8 (z_hi: 4, z_lo: 2; z = z_hi * 2 + z_lo), core: 2. Of those that a mesh axis runs over, the one named last changes fastest.
Arguments:
- prefill_hidden: bfloat16 [8192, 8192], P('section', 'tp'), may hold values from -180 to 180
- norm_gain: float32 [8192], replicated, may hold values from 0.25 to 1.75
- key_weight: bfloat16 [8192, 1024], P(None, 'tp'), may hold values from -0.0625 to 0.0625
- value_weight: bfloat16 [8192, 1024], P(None, 'tp'), may hold values from -0.0625 to 0.0625
- prefill_query: bfloat16 [8192, 8192], P('section', 'tp'), may hold values from -102 to 102
- resident_keys: bfloat16 [8192, 16, 1024], P('section', None, 'tp'), may hold values from -6 to 6
- resident_values: bfloat16 [8192, 16, 1024], P('section', None, 'tp'), may hold values from -6 to 6
- decode_query: bfloat16 [512, 8192], P('section', 'tp'), may hold values from -102 to 102
- page_owner: int32 [512], P('section'), may hold values from 0 to 31, as said below
- block_table: int32 [512, 64], P('section'), may hold values from 0 to 319, as said below
- context_len: int32 [512], P('section'), may hold values from 1 to 1024, as said below
Outputs:
- prefill_attention: bfloat16 [8192, 8192], P('section', 'tp')
- decode_attention: bfloat16 [512, 8192], P('section', 'tp')
Inputs may be any that keep to these rules, and one draw needn't show every extreme that they name: `page_owner`: the 16 pages of each section device go to 8 different owners, exactly 2 pages to each; one owner receives pages from every section device. `block_table`: row entries name first the row's resident pages (below 256), then 256 + page_slot for at most 4 pages sent to the row's owner; every page sent to an owner is named by exactly one of its rows; entries after a row's pages are 0. `context_len`: A row's last visible token lies in the last page its table names.
All inputs are finite; a program needn't handle non-finite values.
Results may differ from a plain program's by a relative error of at most 0.011.
Values may be sent and summed in bfloat16 or wider, within the bound.
A program may use at most 192 MiB of HBM per device.

v0:
```python
import math

import jax
import jax.numpy as jnp
from jax import lax
from jax.sharding import PartitionSpec as P

HD = 128
PAGE = 16
CAP = 2


NORM_EPSILON = 1e-05
ROPE_THETA = 500000.0
NEG_LARGE = -1e30


def rotate_keys(raw_keys, positions):
    head_width = raw_keys.shape[-1]
    half_width = head_width // 2
    frequency = jnp.exp(
        jnp.arange(half_width, dtype=jnp.float32) * (-2.0 * math.log(ROPE_THETA) / head_width)
    )
    angles = positions.astype(jnp.float32)[:, None] * frequency[None, :]
    cosine = jnp.cos(angles)[:, None, :]
    sine_part = jnp.sin(angles)[:, None, :]
    first_half = raw_keys[..., :half_width]
    second_half = raw_keys[..., half_width:]
    return jnp.concatenate(
        [
            first_half * cosine - second_half * sine_part,
            second_half * cosine + first_half * sine_part,
        ],
        axis=-1,
    )


def empty_state(kv_heads, group_size, query_rows, head_width):
    return (
        jnp.full((kv_heads, group_size, query_rows), NEG_LARGE, jnp.float32),
        jnp.zeros((kv_heads, group_size, query_rows), jnp.float32),
        jnp.zeros((kv_heads, group_size, query_rows, head_width), jnp.float32),
    )


def attend_piece(carried, queries, query_pos, key_piece, value_piece, key_pos, score_scale):
    kv_heads = queries.shape[1]
    head_width = queries.shape[3]

    def compute(current):
        row_max, row_sum, weighted = current
        piece_rows = key_piece.shape[0]
        key_block = key_piece.reshape(piece_rows, kv_heads, head_width)
        value_block = value_piece.reshape(piece_rows, kv_heads, head_width)
        scores = (
            jnp.einsum("tkgd,rkd->kgtr", queries, key_block, preferred_element_type=jnp.float32)
            * score_scale
        )
        visible = key_pos[None, :] <= query_pos[:, None]
        scores = jnp.where(visible, scores, NEG_LARGE)
        new_max = jnp.maximum(row_max, jnp.max(scores, axis=-1))
        weights = jnp.where(visible, jnp.exp(scores - new_max[..., None]), 0.0)
        new_sum = jnp.sum(weights, axis=-1)
        product = jnp.einsum(
            "kgtr,rkd->kgtd",
            weights.astype(jnp.bfloat16),
            value_block,
            preferred_element_type=jnp.float32,
        )
        return (new_max, new_sum, product)

    return lax.cond(
        jnp.min(key_pos) > jnp.max(query_pos), lambda current: current, compute, carried
    )


def finish_state(carried):
    row_max, row_sum, weighted = carried
    result = weighted / row_sum[..., None]
    kv_heads, group_size, query_rows, head_width = result.shape
    return (
        jnp.transpose(result, (2, 0, 1, 3))
        .reshape(query_rows, kv_heads * group_size * head_width)
        .astype(jnp.bfloat16)
    )


def per_device(
    prefill_hidden,
    norm_gain,
    key_weight,
    value_weight,
    prefill_query,
    resident_keys,
    resident_values,
    decode_query,
    page_owner,
    block_table,
    context_len,
):
    section_count = lax.axis_size("section")
    section_index = lax.axis_index("section")
    stretch_rows = prefill_hidden.shape[0]
    key_width = key_weight.shape[1]
    head_width = HD
    kv_heads = key_width // head_width
    query_width = prefill_query.shape[1]
    group_size = query_width // key_width
    score_scale = 1.0 / math.sqrt(head_width)
    features = lax.all_gather(prefill_hidden, "tp", axis=1, tiled=True)
    feature_f32 = features.astype(jnp.float32)
    inverse_rms = lax.rsqrt(
        jnp.mean(feature_f32 * feature_f32, axis=1, keepdims=True) + NORM_EPSILON
    )
    normed = (feature_f32 * inverse_rms * norm_gain).astype(jnp.bfloat16)
    raw_keys = jnp.dot(normed, key_weight, preferred_element_type=jnp.float32)
    value_rows = jnp.dot(normed, value_weight, preferred_element_type=jnp.float32).astype(
        jnp.bfloat16
    )
    positions = section_index * stretch_rows + jnp.arange(stretch_rows, dtype=jnp.int32)
    key_rows = (
        rotate_keys(raw_keys.reshape(stretch_rows, kv_heads, head_width), positions)
        .reshape(stretch_rows, key_width)
        .astype(jnp.bfloat16)
    )
    queries = prefill_query.reshape(stretch_rows, kv_heads, group_size, head_width)
    pieces = (
        lax.all_gather(key_rows, "section", axis=0, tiled=True),
        lax.all_gather(value_rows, "section", axis=0, tiled=True),
    )
    key_pos = jnp.arange(pieces[0].shape[0], dtype=jnp.int32)
    folded = attend_piece(
        empty_state(kv_heads, group_size, stretch_rows, head_width),
        queries,
        positions,
        pieces[0],
        pieces[1],
        key_pos,
        score_scale,
    )
    prefill_attention = finish_state(folded)
    pages_here = stretch_rows // PAGE
    page_data = jnp.concatenate([key_rows, value_rows], axis=1).reshape(
        pages_here, PAGE * 2 * key_width
    )
    page_index = jnp.arange(pages_here, dtype=jnp.int32)
    same_owner = (page_owner[:, None] == page_owner[None, :]) & (
        page_index[None, :] < page_index[:, None]
    )
    page_rank = jnp.sum(same_owner.astype(jnp.int32), axis=1)
    slot_index = page_owner * CAP + page_rank
    placement_matrix = (
        jnp.arange(section_count * CAP, dtype=jnp.int32)[:, None] == slot_index[None, :]
    ).astype(jnp.bfloat16)
    outgoing = jnp.dot(placement_matrix, page_data, preferred_element_type=jnp.float32).astype(
        jnp.bfloat16
    )
    outgoing = outgoing.reshape(section_count, CAP, PAGE * 2 * key_width)
    arrived = lax.all_to_all(outgoing, "section", split_axis=0, concat_axis=0, tiled=True).reshape(
        section_count * CAP, PAGE, 2 * key_width
    )
    cache_keys = jnp.concatenate([resident_keys, arrived[:, :, :key_width]], axis=0)
    cache_values = jnp.concatenate([resident_values, arrived[:, :, key_width:]], axis=0)
    decode_rows = decode_query.shape[0]
    key_span = block_table.shape[1] * PAGE
    gathered_keys = cache_keys[block_table].reshape(decode_rows, key_span, kv_heads, head_width)
    gathered_values = cache_values[block_table].reshape(decode_rows, key_span, kv_heads, head_width)
    decode_queries = decode_query.reshape(decode_rows, kv_heads, group_size, head_width)
    scores = (
        jnp.einsum(
            "bkgd,blkd->bkgl", decode_queries, gathered_keys, preferred_element_type=jnp.float32
        )
        * score_scale
    )
    visible = (jnp.arange(key_span, dtype=jnp.int32)[None, :] < context_len[:, None])[
        :, None, None, :
    ]
    scores = jnp.where(visible, scores, NEG_LARGE)
    row_max = jnp.max(scores, axis=-1, keepdims=True)
    weights = jnp.exp(scores - row_max)
    row_sum = jnp.sum(weights, axis=-1, keepdims=True)
    attended = (
        jnp.einsum(
            "bkgl,blkd->bkgd",
            weights.astype(jnp.bfloat16),
            gathered_values,
            preferred_element_type=jnp.float32,
        )
        / row_sum
    )
    decode_attention = attended.reshape(decode_rows, query_width).astype(jnp.bfloat16)
    return (prefill_attention, decode_attention)


def solution(mesh):
    return jax.shard_map(
        per_device,
        mesh=mesh,
        in_specs=(
            P("section", "tp"),
            P(),
            P(None, "tp"),
            P(None, "tp"),
            P("section", "tp"),
            P("section", None, "tp"),
            P("section", None, "tp"),
            P("section", "tp"),
            P("section"),
            P("section", None),
            P("section"),
        ),
        out_specs=(P("section", "tp"), P("section", "tp")),
        check_vma=False,
    )
```

profile of v0, /device:TPU:32, one launch (start us, length us, event | category | flops | bytes accessed | tf_op | source)
XLA Modules:
  0.0 412.8 jit_solution(1083435418822819909)
XLA Ops:
  7.2 0.7 all-gather.5.cloned.1.call-update
  8.0 56.6 %all-gather.5.cloned.1.call-done = bf16[256,8192]{1,0:T(8,128)(2,1)} async-done(((bf16[256,1024]{1,0:T(8,128)(2,1)}), bf16[256,8192]{1,0:T(8,128)(2,1)}) %all-gather.5.cloned.1.call-update) | async-done | bytes 4194320 | tf_op jit(solution)/shard_map/all_gather | solution.py:110
  64.6 3.3 fusion.20
  68.1 1.7 fusion.29
  70.9 5.2 %fusion.32 = bf16[256,128]{0,1:T(8,128)(2,1)} fusion(bf16[8192,128]{1,0:T(8,128)(2,1)} %param.16, bf16[256,8192]{1,0:T(8,128)(2,1)} %all-gather.5.cloned.1.call-done, f32[8192]{0:T(1024)S(1)} %copy-done.7, f32[256]{0:T(256)S(1)} %add_rsqrt_fusion), kind=kOutput, calls=%fused_computation.35 | convolution fusion | flops 545292288 | bytes 6390784 | tf_op jit(solution)/shard_map/dot_general | solution.py:117
  76.4 0.9 pad_maximum_fusion.2
  77.7 1.1 reshape.216
  78.8 8.8 %all-to-all-start = ((bf16[32,2,4096]{2,1,0:T(2,128)(2,1)}), bf16[32,2,4096]{2,1,0:T(2,128)(2,1)S(1)}, u32[]{:S(2)}, u32[]{:S(2)}) async-start(bf16[32,2,4096]{2,1,0:T(2,128)(2,1)} %reshape.216), calls=%async_computation | async-start | bytes 1048576 | tf_op jit(solution)/shard_map/all_to_all | solution.py:159
  87.6 0.6 fusion.52
  89.1 10.8 %all-to-all-done = bf16[32,2,4096]{2,1,0:T(2,128)(2,1)S(1)} async-done(((bf16[32,2,4096]{2,1,0:T(2,128)(2,1)}), bf16[32,2,4096]{2,1,0:T(2,128)(2,1)S(1)}, u32[]{:S(2)}, u32[]{:S(2)}) %all-to-all-start) | async-done | bytes 524320 | tf_op jit(solution)/shard_map/all_to_all | solution.py:159
  100.4 2.8 pad_maximum_fusion
  103.2 9.6 %gather_fusion = bf16[1024,16,128]{2,1,0:T(8,128)(2,1)} fusion(bf16[320,16,128]{2,1,0:T(8,128)(2,1)} %get-tuple-element.49, s32[1024]{0:T(1024)S(1)} %broadcast_clamp_fusion), kind=kCustom, calls=%fused_computation | custom fusion | bytes 8392704 | tf_op jit(solution)/shard_map/gather | solution.py:166
  112.8 8.3 %gather_fusion.1 = bf16[1024,16,128]{2,1,0:T(8,128)(2,1)} fusion(bf16[320,16,128]{2,1,0:T(8,128)(2,1)S(1)} %get-tuple-element.50, s32[1024]{0:T(1024)S(1)} %broadcast_clamp_fusion), kind=kCustom, calls=%fused_computation.1 | custom fusion | bytes 8392704 | tf_op jit(solution)/shard_map/gather | solution.py:167
  121.1 3.6 fusion.55
  125.0 0.7 fusion.35
  125.7 0.6 copy.49
  126.4 71.9 %all-gather.9.cloned.1.call-done = bf16[8192,1,128]{0,2,1:T(8,128)(2,1)} async-done(((bf16[256,1,128]{0,2,1:T(8,128)(2,1)}), bf16[8192,1,128]{0,2,1:T(8,128)(2,1)}) %all-gather.9.cloned.1.call-update) | async-done | bytes 2097168 | tf_op jit(solution)/shard_map/all_gather | solution.py:128
  198.2 126.8 %all-gather.7.cloned.1.call-done = bf16[8192,128]{0,1:T(8,128)(2,1)} async-done(((bf16[256,128]{0,1:T(8,128)(2,1)}), bf16[8192,128]{0,1:T(8,128)(2,1)}) %all-gather.7.cloned.1.call-update) | async-done | bytes 2097168 | tf_op jit(solution)/shard_map/all_gather | solution.py:129
  325.0 79.7 %conditional.1 = (f32[1,8,256]{2,1,0:T(8,128)S(1)}, f32[1,8,256,128]{3,2,1,0:T(8,128)S(1)}) conditional(s32[]{:T(128)} %convert_element_type.52, (s32[8192]{0:T(1024)S(1)}, s32[256]{0:T(256)S(1)}, bf16[256,1024]{1,0:T(8,128)(2,1)S(1)}, bf16[8192,128]{0,1:T(8,128)(2,1)}, bf16[8192,128]{0,1:T(8,128)(2,1)}) %tuple.37, () %tuple.17), branch_computations={%region_2.5_spmd, %region_5.0_spmd} | conditional | flops 8810133504 | bytes 215565328 | solution.py:72
  325.0 4.7 %broadcast_compare_fusion = pred[256,8192]{0,1:T(8,128)(4,1)} fusion(s32[256]{0:T(256)S(1)} %get-tuple-element.12, s32[8192]{0:T(1024)S(1)} %get-tuple-element.11), kind=kLoop, calls=%fused_computation.10 | loop fusion | flops 2097152 | bytes 2130944 | tf_op jit(solution)/shard_map/cond/branch_0_fun/le | solution.py:59
  329.7 25.5 %fusion = (f32[8,256]{1,0:T(8,128)S(1)}, f32[8192,256,8]{1,0,2:T(8,128)}) fusion(pred[256,8192]{0,1:T(8,128)(4,1)} %broadcast_compare_fusion, bf16[8192,128]{0,1:T(8,128)(2,1)} %get-tuple-element.37, bf16[256,1024]{1,0:T(8,128)(2,1)S(1)} %get-tuple-element.23), kind=kOutput, calls=%fused_computation.4 | convolution fusion | flops 4345296896 | bytes 71835648 | tf_op jit(solution)/shard_map/cond/branch_0_fun/tkgd,rkd->kgtr/dot_general | solution.py:56
  355.2 27.2 %fusion.10 = f32[1,8,256,128]{3,2,1,0:T(8,128)S(1)} fusion(bf16[8192,128]{0,1:T(8,128)(2,1)} %get-tuple-element.38, f32[8192,256,8]{1,0,2:T(8,128)} %get-tuple-element.40, f32[8,256]{1,0:T(8,128)S(1)} %broadcast_maximum_fusion, pred[256,8192]{0,1:T(8,128)(4,1)} %broadcast_compare_fusion), kind=kOutput, calls=%fused_computation.14 | convolution fusion | flops 4378853376 | bytes 72359936 | tf_op jit(solution)/shard_map/cond/branch_0_fun/kgtr,rkd->kgtd/dot_general | solution.py:64
  382.4 22.3 %fusion.2 = f32[8,256]{1,0:T(8,128)S(1)} fusion(f32[8192,256,8]{1,0,2:T(8,128)} %get-tuple-element.40, f32[8,256]{1,0:T(8,128)S(1)} %broadcast_maximum_fusion, pred[256,8192]{0,1:T(8,128)(4,1)} %broadcast_compare_fusion), kind=kLoop, calls=%fused_computation.6 | loop fusion | flops 83884032 | bytes 69222400 | tf_op jit(solution)/shard_map/cond/branch_0_fun/reduce_sum | solution.py:63
  405.4 0.9 copy.48
  (46 shorter events, 3.5 us)
Async XLA Ops:
  7.2 60.7 %copy-start = (bf16[8192,128]{1,0:T(8,128)(2,1)S(1)}, bf16[8192,128]{1,0:T(8,128)(2,1)}, u32[]{:S(2)}) copy-start(bf16[8192,128]{1,0:T(8,128)(2,1)} %param.15) | copy-start | bytes 6291460
  7.2 60.7 %copy-start.7 = (f32[8192]{0:T(1024)S(1)}, f32[8192]{0:T(1024)}, u32[]{:S(2)}) copy-start(f32[8192]{0:T(1024)} %param.14) | copy-start | bytes 98308
  7.2 57.4 %all-gather.5.cloned.1.call-start = ((), (), s32[]{:S(2)}) async-start(), calls=%async_computation.1 | async-start | bytes 4718592 | tf_op jit(solution)/shard_map/all_gather | solution.py:110
  7.9 190.3 %all-gather.9.cloned.1.call-start = ((), (), s32[]{:S(2)}) async-start(), calls=%async_computation.3 | async-start | bytes 2162688 | tf_op jit(solution)/shard_map/all_gather | solution.py:128
  64.6 3.4 copy-start.2
  70.8 5.4 %copy-start.8 = (s32[16]{0:T(128)S(1)}, s32[16]{0:T(128)}, u32[]{:S(2)}) copy-start(s32[16]{0:T(128)} %param.21) | copy-start | bytes 196
  70.8 17.4 %copy-start.4 = (s32[16,64]{1,0:T(8,128)S(1)}, s32[16,64]{1,0:T(8,128)}, u32[]{:S(2)}) copy-start(s32[16,64]{1,0:T(8,128)} %param.22) | copy-start | bytes 12292
  70.8 17.5 %copy-start.3 = (bf16[16,1024]{1,0:T(8,128)(2,1)S(1)}, bf16[16,1024]{1,0:T(8,128)(2,1)}, u32[]{:S(2)}) copy-start(bf16[16,1024]{1,0:T(8,128)(2,1)} %param.20) | copy-start | bytes 98308
  70.8 18.2 %copy-start.5 = (s32[16]{0:T(128)S(1)}, s32[16]{0:T(128)}, u32[]{:S(2)}) copy-start(s32[16]{0:T(128)} %param.23) | copy-start | bytes 196
  70.9 254.2 %all-gather.7.cloned.1.call-start = ((), (), s32[]{:S(2)}) async-start(), calls=%async_computation.2 | async-start | bytes 2162688 | tf_op jit(solution)/shard_map/all_gather | solution.py:129
  78.8 21.1 %all-to-all-start = ((bf16[32,2,4096]{2,1,0:T(2,128)(2,1)}), bf16[32,2,4096]{2,1,0:T(2,128)(2,1)S(1)}, u32[]{:S(2)}, u32[]{:S(2)}) async-start(bf16[32,2,4096]{2,1,0:T(2,128)(2,1)} %reshape.216), calls=%async_computation | async-start | bytes 1048576 | tf_op jit(solution)/shard_map/all_to_all | solution.py:159
  121.1 3.9 copy-start.1
  121.1 203.9 %copy-start.6 = (bf16[256,1024]{1,0:T(8,128)(2,1)S(1)}, bf16[256,1024]{1,0:T(8,128)(2,1)}, u32[]{:S(2)}) copy-start(bf16[256,1024]{1,0:T(8,128)(2,1)} %param.17) | copy-start | bytes 1572868
Sparse Core Ops, SparseCore 0:
  9.8 54.7 all-gather.4
  70.9 127.2 all-gather.8
  199.9 125.0 all-gather.6
where the time goes:
time: 413 us
  waiting for transfers between devices  267 us (65%)
  matrix products  64.3 us (16%)
  other arithmetic  36.3 us (9%)
  local copies, waits for them, and re-layouts  21.8 us (5%)
  between operations  14.6 us (4%)
  starting transfers between devices  8.9 us (2%)
    all_gather x1, waiting for transfers between devices, per_device(): lax.all_gather(value_rows, 'section', axis=0, tiled=True)  127 us
    all_gather x1, waiting for transfers between devices, per_device(): lax.all_gather(key_rows, 'section', axis=0, tiled=True)  71.9 us
    all_gather x1, waiting for transfers between devices, per_device(): features = lax.all_gather(prefill_hidden, 'tp', axis=1, tiled=True)  56.6 us
    dot_general x1, matrix products, compute(): jnp.einsum('kgtr,rkd->kgtd', weights.astype(jnp.bfloat16), value_block, p...  27.2 us
    dot_general x1, matrix products, compute(): jnp.einsum('tkgd,rkd->kgtr', queries, key_block, preferred_element_type=j...  25.5 us
    reduce_sum x1, other arithmetic, compute(): new_sum = jnp.sum(weights, axis=-1)  22.3 us
    all_to_all x1, waiting for transfers between devices, per_device(): lax.all_to_all(outgoing, 'section', split_axis=0, concat_axis=0, tiled=True)  10.8 us
    gather x1, local copies, waits for them, and re-layouts, per_device(): cache_keys[block_table].reshape(decode_rows, key_span, kv_heads, head_width)  9.6 us
  transfers between devices with their start and end apart: 4, of which 4 were waited for; matrix products, arithmetic and copies ran while one was open for 8% of the time, Pallas kernels for 0%

commit v1 on v0

v1 whole, which is shorter than its diff:
```python
import functools
import math

import numpy as np

import jax
import jax.numpy as jnp
from jax import lax
from jax.experimental import pallas as pl
from jax.experimental.pallas import tpu as pltpu
from jax.sharding import PartitionSpec as P

MESH = pl.DeviceIdType.MESH
HD = 128
PAGE = 16
NORM_EPSILON = 1e-05
ROPE_THETA = 500000.0
NEG = -1e30
CHUNKS = 4
TILE_Y = 4
UNIT_HEADS = 2
N_COPIES = 26
N_META = 9
POW = math.log2(math.e) / math.sqrt(HD)

NT = (((1,), (1,)), ((), ()))
TN = (((0,), (0,)), ((), ()))


def rope_tables(stretch, sections):
    half = HD // 2
    exponent = np.arange(half, dtype=np.float32) * np.float32(-2.0 * math.log(ROPE_THETA) / HD)
    frequency = np.exp(exponent).astype(np.float64)
    inner = np.arange(stretch)[:, None] * frequency[None, :]
    outer = (np.arange(sections) * stretch)[:, None] * frequency[None, :]

    def both(angles):
        cosine = np.concatenate([np.cos(angles), np.cos(angles)], axis=1)
        sine = np.concatenate([np.sin(angles), np.sin(angles)], axis=1)
        return cosine.astype(np.float32), sine.astype(np.float32)

    return both(inner) + both(outer)


def kernel(
    hidden,
    gain,
    key_weight,
    value_weight,
    query,
    resident_keys,
    resident_values,
    decode_query,
    owner,
    table,
    context,
    cos_in,
    sin_in,
    cos_out,
    sin_out,
    out,
    decode_out,
    hid,
    wkv,
    kb,
    vb,
    meta,
    qs,
    rk,
    rv,
    dqm,
    cosine,
    sine,
    row_max,
    row_sum,
    acc,
    visible_pages,
    last_page,
    count_full,
    count_last,
    dec_max,
    dec_sum,
    dec_acc,
    local_sem,
    send_sem,
    recv_sem,
    meta_send,
    meta_recv,
):
    stretch = hidden.shape[0]
    width = hidden.shape[1]
    chunks = kb.shape[0]
    rows = stretch // chunks
    half_rows = rows // 2
    heads = qs.shape[0]
    pages_chunk = rows // PAGE
    pages_here = stretch // PAGE
    pool = rk.shape[0]
    max_pages = table.shape[1]
    decode_rows = decode_query.shape[0]
    lanes = 128

    s = lax.axis_index("section")
    t = lax.axis_index("tp")
    zh, core = t // 2, t % 2
    zl, y, x = s // 16, (s // 4) % 4, s % 4
    t_r, t_l, t_o = ((zh + 1) % 4) * 2 + core, ((zh + 3) % 4) * 2 + core, ((zh + 2) % 4) * 2 + core
    other = 1 - core
    t_p = zh * 2 + other
    p_r, p_l, p_o = ((zh + 1) % 4) * 2 + other, ((zh + 3) % 4) * 2 + other, ((zh + 2) % 4) * 2 + other
    xp, xm, xo = (x + 1) % 4, (x + 3) % 4, (x + 2) % 4
    yp, ym, yo = (y + 1) % 4, (y + 3) % 4, (y + 2) % 4
    zo = 1 - zl

    def at_section(zz, yy, xx):
        return (zz * 16 + yy * 4 + xx, t)

    z_right, z_left, partner = (s, t_r), (s, t_l), (s, t_p)
    z_other = at_section(zo, y, x)
    x_right, x_left = at_section(zl, y, xp), at_section(zl, y, xm)
    y_up, y_down = at_section(zl, yp, x), at_section(zl, ym, x)

    every = slice(None)

    def routes(c):
        top, bottom = pl.ds(0, half_rows), pl.ds(half_rows, half_rows)
        mine = hidden.at[pl.ds(pl.multiple_of(c * rows, rows), rows), :]
        return (
            (mine, hid.at[c, t], hid.at[c, t_l], z_right),
            (mine, hid.at[c, t], hid.at[c, t_r], z_left),
            (hid.at[c, t_l, top], hid.at[c, t_l, top], hid.at[c, t_o, top], z_right),
            (hid.at[c, t_r, bottom], hid.at[c, t_r, bottom], hid.at[c, t_o, bottom], z_left),
            (mine, hid.at[c, t], hid.at[c, t_p], partner),
            (hid.at[c, t_l], hid.at[c, t_l], hid.at[c, p_l], partner),
            (hid.at[c, t_r], hid.at[c, t_r], hid.at[c, p_r], partner),
            (hid.at[c, t_o], hid.at[c, t_o], hid.at[c, p_o], partner),
            (kb.at[c, zl, y, x], kb.at[c, zl, y, x], kb.at[c, zo, y, x], z_other),
            (vb.at[c, zl, y, x], vb.at[c, zl, y, x], vb.at[c, zo, y, x], z_other),
            (kb.at[c, :, y, x], kb.at[c, :, y, x], kb.at[c, :, y, xm], x_right),
            (kb.at[c, :, y, x], kb.at[c, :, y, x], kb.at[c, :, y, xp], x_left),
            (vb.at[c, :, y, x], vb.at[c, :, y, x], vb.at[c, :, ym, x], y_up),
            (vb.at[c, :, y, x], vb.at[c, :, y, x], vb.at[c, :, yp, x], y_down),
            (kb.at[c, 0, y, xm], kb.at[c, 0, y, xm], kb.at[c, 0, y, xo], x_right),
            (kb.at[c, 1, y, xp], kb.at[c, 1, y, xp], kb.at[c, 1, y, xo], x_left),
            (vb.at[c, 0, ym, x], vb.at[c, 0, ym, x], vb.at[c, 0, yo, x], y_up),
            (vb.at[c, 1, yp, x], vb.at[c, 1, yp, x], vb.at[c, 1, yo, x], y_down),
            (kb.at[c, :, y], kb.at[c, :, y], kb.at[c, :, ym], y_up),
            (kb.at[c, :, y], kb.at[c, :, y], kb.at[c, :, yp], y_down),
            (vb.at[c, :, :, x], vb.at[c, :, :, x], vb.at[c, :, :, xm], x_right),
            (vb.at[c, :, :, x], vb.at[c, :, :, x], vb.at[c, :, :, xp], x_left),
            (kb.at[c, 0, ym], kb.at[c, 0, ym], kb.at[c, 0, yo], y_up),
            (kb.at[c, 1, yp], kb.at[c, 1, yp], kb.at[c, 1, yo], y_down),
            (vb.at[c, 0, :, xm], vb.at[c, 0, :, xm], vb.at[c, 0, :, xo], x_right),
            (vb.at[c, 1, :, xp], vb.at[c, 1, :, xp], vb.at[c, 1, :, xo], x_left),
        )

    meta_routes = (
        (meta.at[zl, y, x], meta.at[zo, y, x], z_other),
        (meta.at[:, y, x], meta.at[:, y, xm], x_right),
        (meta.at[:, y, x], meta.at[:, y, xp], x_left),
        (meta.at[0, y, xm], meta.at[0, y, xo], x_right),
        (meta.at[1, y, xp], meta.at[1, y, xo], x_left),
        (meta.at[:, y], meta.at[:, ym], y_up),
        (meta.at[:, y], meta.at[:, yp], y_down),
        (meta.at[0, ym], meta.at[0, yo], y_up),
        (meta.at[1, yp], meta.at[1, yo], y_down),
    )

    def remote(c, k):
        source, target, _, device = routes(c)[k]
        return pltpu.make_async_remote_copy(
            src_ref=source,
            dst_ref=target,
            send_sem=send_sem.at[c, k],
            recv_sem=recv_sem.at[c, k],
            device_id=device,
            device_id_type=MESH,
        )

    def arrival(c, k):
        _, _, landing, device = routes(c)[k]
        return pltpu.make_async_remote_copy(
            src_ref=landing,
            dst_ref=landing,
            send_sem=send_sem.at[c, k],
            recv_sem=recv_sem.at[c, k],
            device_id=device,
            device_id_type=MESH,
        )

    def start(c, *ks):
        for k in ks:
            remote(c, k).start()

    def await_arrival(c, *ks):
        for k in ks:
            arrival(c, k).wait_recv()

    def meta_copy(k):
        source, _, device = meta_routes[k]
        return pltpu.make_async_remote_copy(
            src_ref=source,
            dst_ref=source,
            send_sem=meta_send.at[k],
            recv_sem=meta_recv.at[k],
            device_id=device,
            device_id_type=MESH,
        )

    def meta_arrival(k):
        _, landing, device = meta_routes[k]
        return pltpu.make_async_remote_copy(
            src_ref=landing,
            dst_ref=landing,
            send_sem=meta_send.at[k],
            recv_sem=meta_recv.at[k],
            device_id=device,
            device_id_type=MESH,
        )

    def meta_start(*ks):
        for k in ks:
            meta_copy(k).start()

    def meta_await(*ks):
        for k in ks:
            meta_arrival(k).wait_recv()

    own_hidden = [
        pltpu.make_async_copy(
            hidden.at[pl.ds(c * rows, rows), :], hid.at[c, t], local_sem.at[c]
        )
        for c in range(chunks)
    ]
    weights_in = [
        pltpu.make_async_copy(key_weight, wkv.at[:, pl.ds(0, lanes)], local_sem.at[chunks]),
        pltpu.make_async_copy(value_weight, wkv.at[:, pl.ds(lanes, lanes)], local_sem.at[chunks + 1]),
    ]
    resident_in = [
        pltpu.make_async_copy(resident_keys, rk, local_sem.at[chunks + 2]),
        pltpu.make_async_copy(resident_values, rv, local_sem.at[chunks + 3]),
    ]
    query_in = [
        pltpu.make_async_copy(
            query.at[:, pl.ds(h * lanes, lanes)], qs.at[h], local_sem.at[chunks + 4 + h]
        )
        for h in range(heads)
    ]

    neighbours = (z_right, z_left, partner, z_other, x_right, x_left, y_up, y_down)
    barrier = pltpu.get_barrier_semaphore()
    for device in neighbours:
        pl.semaphore_signal(barrier, inc=1, device_id=device, device_id_type=MESH)
    for copy in own_hidden + resident_in + weights_in + query_in:
        copy.start()
    pl.semaphore_wait(barrier, len(neighbours))

    for c in range(2):
        start(c, 0, 1, 4)

    owners = [owner[i] for i in range(pages_here)]
    page_row = lax.broadcasted_iota(jnp.int32, (pages_here, lanes), 0)
    codes = jnp.zeros((pages_here, lanes), jnp.int32)
    for i in range(pages_here):
        rank = jnp.int32(0)
        for j in range(i):
            rank = rank + jnp.where(owners[j] == owners[i], 1, 0).astype(jnp.int32)
        code = owners[i] * 64 + s * 2 + rank
        codes = jnp.where(page_row == i, code, codes)
    meta[zl, y, x] = codes

    lane_row = lax.broadcasted_iota(jnp.int32, (1, lanes), 1) % decode_rows
    lengths = jnp.zeros((1, lanes), jnp.int32)
    for r in range(decode_rows):
        lengths = jnp.where(lane_row == r, context[r], lengths)
    full_pages = lax.shift_right_logical(lengths - 1, 4)
    last_tokens = lengths - full_pages * PAGE
    last_page[...] = jnp.zeros((1, lanes), jnp.int32)

    def table_row(j, carry):
        entries = jnp.zeros((1, lanes), jnp.int32)
        for r in range(decode_rows):
            entries = jnp.where(lane_row == r, table[r, j], entries)
        visible_pages[pl.ds(j, 1), :] = jnp.where(full_pages > j, entries, -1)
        last_page[...] = jnp.where(full_pages == j, entries, last_page[...])
        return carry

    lax.fori_loop(0, max_pages, table_row, 0)
    meta_start(0)

    for h in range(heads):
        dqm[h * decode_rows : (h + 1) * decode_rows, :] = decode_query[:, h * lanes : (h + 1) * lanes]
    ca, sa = cos_out[pl.ds(s, 1), :], sin_out[pl.ds(s, 1), :]
    low = lax.broadcasted_iota(jnp.int32, (1, lanes), 1) < lanes // 2
    cosine[...] = ca * cos_in[...] - sa * sin_in[...]
    sine[...] = jnp.where(low, -1.0, 1.0) * (sa * cos_in[...] + ca * sin_in[...])
    row_max[...] = jnp.full(row_max.shape, NEG, jnp.float32)
    row_sum[...] = jnp.zeros(row_sum.shape, jnp.float32)
    acc[...] = jnp.zeros(acc.shape, jnp.float32)
    dec_max[...] = jnp.full(dec_max.shape, NEG, jnp.float32)
    dec_sum[...] = jnp.zeros(dec_sum.shape, jnp.float32)
    dec_acc[...] = jnp.zeros(dec_acc.shape, jnp.float32)

    def count_pages(page_ids):
        def step(j, total):
            return total + jnp.where(page_ids == visible_pages[pl.ds(j, 1), :], 1.0, 0.0)

        total = lax.fori_loop(
            0, max_pages, step, jnp.zeros(page_ids.shape, jnp.float32), unroll=8
        )
        return total, jnp.where(page_ids == last_page[...], 1.0, 0.0)

    def decode_tile(keys, values, counts):
        scores = lax.dot_general(keys, dqm[...], NT, preferred_element_type=jnp.float32)
        scores = jnp.where(counts > 0.0, scores, NEG)
        old = dec_max[...]
        new = jnp.maximum(old, jnp.max(scores, axis=0, keepdims=True))
        weights = counts * jnp.exp2((scores - new) * POW)
        shrink = jnp.exp2((old - new) * POW)
        dec_max[...] = new
        dec_sum[...] = dec_sum[...] * shrink + jnp.sum(weights, axis=0, keepdims=True)
        dec_acc[...] = dec_acc[...] * shrink + lax.dot_general(
            values, weights.astype(jnp.bfloat16), TN, preferred_element_type=jnp.float32
        )

    for copy in resident_in:
        copy.wait()
    tile_pages = 32
    token_of = lax.broadcasted_iota(jnp.int32, (PAGE, lanes), 0)
    in_last = jnp.where(token_of < last_tokens, 1.0, 0.0)

    def resident_tile(i, carry):
        first = pl.multiple_of(i * tile_pages, tile_pages)
        ids = first + lax.broadcasted_iota(jnp.int32, (tile_pages, lanes), 0)
        total, last = count_pages(ids)
        counts = [
            jnp.broadcast_to(total[p : p + 1, :], (PAGE, lanes))
            + in_last * jnp.broadcast_to(last[p : p + 1, :], (PAGE, lanes))
            for p in range(tile_pages)
        ]
        decode_tile(
            rk[pl.ds(first, tile_pages)].reshape(tile_pages * PAGE, lanes),
            rv[pl.ds(first, tile_pages)].reshape(tile_pages * PAGE, lanes),
            jnp.concatenate(counts, axis=0),
        )
        return carry

    lax.fori_loop(0, pool // tile_pages, resident_tile, 0)

    def count_incoming():
        def one(i, carry):
            for yy in range(4):
                code = meta[i // 4, yy, i % 4] - s * 64
                ids = jnp.where((code >= 0) & (code < 64), code + pool, -5)
                total, last = count_pages(ids)
                sec = (i // 4) * 16 + yy * 4 + i % 4
                count_full[sec] = total
                count_last[sec] = last
            return carry

        lax.fori_loop(0, 8, one, 0)

    def decode_chunk(c):
        def one(i, carry):
            zz, yy = i // 4, i % 4
            counts = []
            for xx in range(4):
                for p in range(pages_chunk):
                    at = pl.ds(c * pages_chunk + p, 1)
                    counts.append(
                        jnp.broadcast_to(count_full[i * 4 + xx, at, :], (PAGE, lanes))
                        + in_last * jnp.broadcast_to(count_last[i * 4 + xx, at, :], (PAGE, lanes))
                    )
            decode_tile(
                kb[c, zz, yy].reshape(4 * rows, lanes),
                vb[c, zz, yy].reshape(4 * rows, lanes),
                jnp.concatenate(counts, axis=0),
            )
            return carry

        lax.fori_loop(0, 8, one, 0)

    shards = hid.shape[1]

    def project(c):
        squares = jnp.zeros((rows, 1), jnp.float32)
        for j in range(shards):
            block = hid[c, j].astype(jnp.float32)
            squares = squares + jnp.sum(block * block, axis=1, keepdims=True)
        inverse = lax.rsqrt(squares * (1.0 / (shards * width)) + NORM_EPSILON)
        total = jnp.zeros((rows, 2 * lanes), jnp.float32)
        for j in range(shards):
            block = hid[c, j].astype(jnp.float32)
            normed = (block * inverse * gain[:, j * width : (j + 1) * width]).astype(jnp.bfloat16)
            total = total + jnp.dot(
                normed, wkv[j * width : (j + 1) * width, :], preferred_element_type=jnp.float32
            )
        keys = total[:, :lanes]
        at = pl.ds(pl.multiple_of(c * rows, rows), rows)
        keys = keys * cosine[at, :] + pltpu.roll(keys, lanes // 2, 1) * sine[at, :]
        kb[c, zl, y, x] = keys.astype(jnp.bfloat16)
        vb[c, zl, y, x] = total[:, lanes:].astype(jnp.bfloat16)

    tile_sections = 4 * TILE_Y
    tile_keys = tile_sections * rows
    tiles = 32 // tile_sections
    own_tile = s // tile_sections

    def attend(c, kt, hp, masked):
        first_y = kt * TILE_Y
        keys = kb[c, first_y // 4, pl.ds(first_y % 4, TILE_Y)].reshape(tile_keys, lanes)
        values = vb[c, first_y // 4, pl.ds(first_y % 4, TILE_Y)].reshape(tile_keys, lanes)
        if masked:
            n = lax.broadcasted_iota(jnp.int32, (stretch, lanes), 1)
            query_pos = s * stretch + lax.broadcasted_iota(jnp.int32, (stretch, lanes), 0)
        for i in range(UNIT_HEADS):
            h = hp * UNIT_HEADS + i
            scores = lax.dot_general(qs[h], keys, NT, preferred_element_type=jnp.float32)
            pieces = [scores[:, j * lanes : (j + 1) * lanes] for j in range(tile_keys // lanes)]
            if masked:
                for j in range(len(pieces)):
                    at = j * lanes + n
                    key_pos = (kt * tile_sections + at // rows) * stretch + c * rows + at % rows
                    pieces[j] = jnp.where(key_pos <= query_pos, pieces[j], NEG)
            top = functools.reduce(jnp.maximum, pieces)
            old = row_max[h]
            new = jnp.maximum(old, jnp.max(top, axis=1, keepdims=True))
            shrink = jnp.exp2((old - new) * POW)
            weights = [jnp.exp2((piece - new) * POW) for piece in pieces]
            row_max[h] = new
            row_sum[h] = row_sum[h] * shrink + functools.reduce(jnp.add, weights)
            weights = jnp.concatenate([w.astype(jnp.bfloat16) for w in weights], axis=1)
            acc[h] = acc[h] * shrink + jnp.dot(weights, values, preferred_element_type=jnp.float32)

    head_units = heads // UNIT_HEADS
    units = tiles * head_units
    segments = 4

    def first_hop(c):
        await_arrival(c, 0, 1)
        start(c, 2, 3, 5, 6)

        @pl.when(c + 2 < chunks)
        def _():
            start(c + 2, 0, 1, 4)

    def second_hop(c):
        await_arrival(c, 2, 3)
        start(c, 7)

    for copy in own_hidden + weights_in + query_in:
        copy.wait()
    first_hop(0)
    second_hop(0)

    def live(c):
        return (c >= 0) & (c < chunks)

    def segment(g, carry):
        period, seg = g // segments, g % segments
        ready = period - 2

        @pl.when((seg == 0) & live(ready))
        def _():
            await_arrival(ready, 22, 23, 24, 25)

            @pl.when(ready == 0)
            def _():
                meta_await(7, 8)

        @pl.when((seg == 1) & live(period))
        def _():
            c = period
            await_arrival(c, 4, 5, 6, 7)
            project(c)
            start(c, 8, 9)

        @pl.when((seg == 1) & live(period - 1))
        def _():
            c = period - 1
            await_arrival(c, 14, 15, 16, 17)
            start(c, 18, 19, 20, 21)

            @pl.when(c == 0)
            def _():
                meta_await(3, 4)
                meta_start(5, 6)

        @pl.when((seg == 2) & live(period + 1))
        def _():
            first_hop(period + 1)

        @pl.when((seg == 2) & live(period))
        def _():
            c = period
            await_arrival(c, 8, 9)
            start(c, 10, 11, 12, 13)

            @pl.when(c == 0)
            def _():
                meta_await(0)
                meta_start(1, 2)

        @pl.when((seg == 3) & live(period - 1))
        def _():
            c = period - 1
            await_arrival(c, 18, 19, 20, 21)
            start(c, 22, 23, 24, 25)

            @pl.when(c == 0)
            def _():
                meta_await(5, 6)
                meta_start(7, 8)

        @pl.when((seg == 3) & live(period))
        def _():
            c = period
            await_arrival(c, 10, 11, 12, 13)
            start(c, 14, 15, 16, 17)

            @pl.when(c == 0)
            def _():
                meta_await(1, 2)
                meta_start(3, 4)

        @pl.when((seg == 3) & live(period + 1))
        def _():
            second_hop(period + 1)

        @pl.when(live(ready))
        def _():
            def one(u, inner):
                kt, hp = u // head_units, u % head_units

                @pl.when(kt < own_tile)
                def _():
                    attend(ready, kt, hp, False)

                @pl.when(kt == own_tile)
                def _():
                    attend(ready, kt, hp, True)

                return inner

            lax.fori_loop(seg * units // segments, (seg + 1) * units // segments, one, 0)

        @pl.when((seg == segments - 1) & live(ready))
        def _():
            @pl.when(ready == 0)
            def _():
                count_incoming()

            decode_chunk(ready)

        return carry

    lax.fori_loop(0, (chunks + 2) * segments, segment, 0)

    for h in range(heads):
        total = jnp.sum(row_sum[h], axis=1, keepdims=True)
        out[:, h * lanes : (h + 1) * lanes] = (acc[h] / total).astype(out.dtype)
    decoded = jnp.transpose(dec_acc[...] / dec_sum[...])
    for h in range(heads):
        decode_out[:, h * lanes : (h + 1) * lanes] = decoded[
            h * decode_rows : (h + 1) * decode_rows, :
        ].astype(decode_out.dtype)

    def drain(c, carry):
        for k in range(N_COPIES):
            remote(c, k).wait_send()
        return carry

    lax.fori_loop(0, chunks, drain, 0)
    for k in range(N_META):
        meta_copy(k).wait_send()


def per_device(
    prefill_hidden,
    norm_gain,
    key_weight,
    value_weight,
    prefill_query,
    resident_keys,
    resident_values,
    decode_query,
    page_owner,
    block_table,
    context_len,
):
    stretch, width = prefill_hidden.shape
    heads = prefill_query.shape[1] // HD
    pool = resident_keys.shape[0]
    features = key_weight.shape[0]
    rows = stretch // CHUNKS
    tables = [jnp.asarray(each) for each in rope_tables(stretch, 32)]
    anywhere = pl.BlockSpec(memory_space=pl.ANY)
    vmem = pl.BlockSpec(memory_space=pltpu.VMEM)
    smem = pl.BlockSpec(memory_space=pltpu.SMEM)
    f32, bf16, i32 = jnp.float32, jnp.bfloat16, jnp.int32
    return pl.pallas_call(
        kernel,
        out_shape=(
            jax.ShapeDtypeStruct(prefill_query.shape, bf16),
            jax.ShapeDtypeStruct(decode_query.shape, bf16),
        ),
        in_specs=[
            anywhere,
            vmem,
            anywhere,
            anywhere,
            anywhere,
            anywhere,
            anywhere,
            vmem,
            smem,
            smem,
            smem,
            vmem,
            vmem,
            vmem,
            vmem,
        ],
        out_specs=(vmem, vmem),
        scratch_shapes=[
            pltpu.VMEM((CHUNKS, features // width, rows, width), bf16),
            pltpu.VMEM((features, 2 * HD), bf16),
            pltpu.VMEM((CHUNKS, 2, 4, 4, rows, HD), bf16),
            pltpu.VMEM((CHUNKS, 2, 4, 4, rows, HD), bf16),
            pltpu.VMEM((2, 4, 4, stretch // PAGE, HD), i32),
            pltpu.VMEM((heads, stretch, HD), bf16),
            pltpu.VMEM((pool, PAGE, HD), bf16),
            pltpu.VMEM((pool, PAGE, HD), bf16),
            pltpu.VMEM((heads * decode_query.shape[0], HD), bf16),
            pltpu.VMEM((stretch, HD), f32),
            pltpu.VMEM((stretch, HD), f32),
            pltpu.VMEM((heads, stretch, HD), f32),
            pltpu.VMEM((heads, stretch, HD), f32),
            pltpu.VMEM((heads, stretch, HD), f32),
            pltpu.VMEM((block_table.shape[1], HD), i32),
            pltpu.VMEM((1, HD), i32),
            pltpu.VMEM((32, stretch // PAGE, HD), f32),
            pltpu.VMEM((32, stretch // PAGE, HD), f32),
            pltpu.VMEM((1, HD), f32),
            pltpu.VMEM((1, HD), f32),
            pltpu.VMEM((HD, HD), f32),
            pltpu.SemaphoreType.DMA((CHUNKS + 4 + heads,)),
            pltpu.SemaphoreType.DMA((CHUNKS, N_COPIES)),
            pltpu.SemaphoreType.DMA((CHUNKS, N_COPIES)),
            pltpu.SemaphoreType.DMA((N_META,)),
            pltpu.SemaphoreType.DMA((N_META,)),
        ],
        compiler_params=pltpu.CompilerParams(
            collective_id=0, has_side_effects=True, vmem_limit_bytes=60 * 1024 * 1024
        ),
        name="attention_layer",
    )(
        prefill_hidden,
        norm_gain.reshape(1, features),
        key_weight,
        value_weight,
        prefill_query,
        resident_keys,
        resident_values,
        decode_query,
        page_owner,
        block_table,
        context_len,
        *tables,
    )


def solution(mesh):
    return jax.shard_map(
        per_device,
        mesh=mesh,
        in_specs=(
            P("section", "tp"),
            P(),
            P(None, "tp"),
            P(None, "tp"),
            P("section", "tp"),
            P("section", None, "tp"),
            P("section", None, "tp"),
            P("section", "tp"),
            P("section"),
            P("section", None),
            P("section"),
        ),
        out_specs=(P("section", "tp"), P("section", "tp")),
        check_vma=False,
    )
```

time: 413 us -> 119 us (0.29)
  waiting for transfers between devices: 267 us -> 0 us
  Pallas kernels: 0 us -> 115 us
  matrix products: 64.3 us -> 0 us
  other arithmetic: 36.3 us -> 0 us
  local copies, waits for them, and re-layouts: 21.8 us -> 3.24 us
  between operations: 14.6 us -> 0.64 us
  starting transfers between devices: 8.9 us -> 0 us
    all_gather x3 -> x0, waiting for transfers between devices: 255 us -> none  [the longest x1 127 us: per_device(): lax.all_gather(value_rows, 'section', axis=0, tiled=True)]
    pallas_call x0 -> x1, Pallas kernels: none -> 115 us  [per_device(): pl.pallas_call(kernel, out_shape=(jax.ShapeDtypeStruct(prefill_query.shap...]
    dot_general x7 -> x0, matrix products: 64.3 us -> none  [the longest x1 27.2 us: compute(): jnp.einsum('kgtr,rkd->kgtd', weights.astype(jnp.bfloat16), value_block, p...]
    reduce_sum x4 -> x0, other arithmetic: 25.9 us -> none  [the longest x1 22.3 us: compute(): new_sum = jnp.sum(weights, axis=-1)]
    gather x2 -> x0, local copies, waits for them, and re-layouts: 17.9 us -> none  [the longest x1 9.6 us: per_device(): cache_keys[block_table].reshape(decode_rows, key_span, kv_heads, head_width)]
    all_to_all x1 -> x0, waiting for transfers between devices: 10.8 us -> none  [per_device(): lax.all_to_all(outgoing, 'section', split_axis=0, concat_axis=0, tiled=True)]
    all_to_all x1 -> x0, starting transfers between devices: 8.79 us -> none  [per_device(): lax.all_to_all(outgoing, 'section', split_axis=0, concat_axis=0, tiled=True)]
    le x1 -> x0, other arithmetic: 4.68 us -> none  [compute(): visible = key_pos[None, :] <= query_pos[:, None]]
  transfers between devices with their start and end apart: 4 -> 0, of which waited for: 4 -> 0; matrix products, arithmetic and copies ran while one was open for 8% -> 0% of each run, Pallas kernels for 0% -> 0%
where the time goes in v1:
time: 119 us
  Pallas kernels  115 us (97%)
  local copies, waits for them, and re-layouts  3.24 us (3%)
    pallas_call x1, Pallas kernels, per_device(): pl.pallas_call(kernel, out_shape=(jax.ShapeDtypeStruct(prefill_query.shap...  115 us
    unnamed x2, local copies, waits for them, and re-layouts  3.24 us

profile of v1, /device:TPU:32, one launch (start us, length us, event | category | flops | bytes accessed | tf_op | source)
XLA Modules:
  0.0 119.2 jit_solution(10648659436811174041)
XLA Ops:
  0.6 115.3 %attention_layer.1 = (bf16[256,1024]{1,0:T(8,128)(2,1)}, bf16[16,1024]{1,0:T(8,128)(2,1)}) custom-call(bf16[256,1024]{1,0:T(8,128)(2,1)} %hidden.1, f32[1,8192]{1,0:T(1,128)} %bitcast.1, bf16[8192,128]{1,0:T(8,128)(2,1)} %key_weight.1, bf16[8192,128]{1,0:T(8,128)(2,1)} %value_weight.1, bf16[256,1024]{1,0:T(8,128)(2,1)} %query.1, ...), custom_call_target="tpu_custom_call" | custom-call | tf_op jit(solution)/shard_map/attention_layer/pallas_call | solution.py:601
  115.9 1.9 %copy.19 = bf16[256,1024]{1,0:T(8,128)(2,1)} copy(bf16[256,1024]{1,0:T(8,128)(2,1)} %get-tuple-element.4) | data formatting | bytes 1048576
  117.8 1.4 %copy.20 = bf16[16,1024]{1,0:T(8,128)(2,1)} copy(bf16[16,1024]{1,0:T(8,128)(2,1)} %get-tuple-element.5) | data formatting | bytes 65536

commit v2 on v1

--- a/solution.py
+++ b/solution.py
@@ -16,11 +16,14 @@
 NORM_EPSILON = 1e-05
 ROPE_THETA = 500000.0
 NEG = -1e30
-CHUNKS = 4
+CHUNKS = 8
 TILE_Y = 4
-UNIT_HEADS = 2
-N_COPIES = 26
-N_META = 9
+UNIT_HEADS = 4
+GROUP = 2
+LAG = 6
+AHEAD = 2
+N_COPIES = 22
+N_META = 7
 POW = math.log2(math.e) / math.sqrt(HD)
 
 NT = (((1,), (1,)), ((), ()))
@@ -78,6 +81,8 @@
     last_page,
     count_full,
     count_last,
+    page_full,
+    page_last,
     dec_max,
     dec_sum,
     dec_acc,
@@ -119,8 +124,7 @@
     z_other = at_section(zo, y, x)
     x_right, x_left = at_section(zl, y, xp), at_section(zl, y, xm)
     y_up, y_down = at_section(zl, yp, x), at_section(zl, ym, x)
-
-    every = slice(None)
+    x_far, y_far = at_section(zl, y, xo), at_section(zl, yo, x)
 
     def routes(c):
         top, bottom = pl.ds(0, half_rows), pl.ds(half_rows, half_rows)
@@ -138,32 +142,26 @@
             (vb.at[c, zl, y, x], vb.at[c, zl, y, x], vb.at[c, zo, y, x], z_other),
             (kb.at[c, :, y, x], kb.at[c, :, y, x], kb.at[c, :, y, xm], x_right),
             (kb.at[c, :, y, x], kb.at[c, :, y, x], kb.at[c, :, y, xp], x_left),
+            (kb.at[c, :, y, x], kb.at[c, :, y, x], kb.at[c, :, y, xo], x_far),
             (vb.at[c, :, y, x], vb.at[c, :, y, x], vb.at[c, :, ym, x], y_up),
             (vb.at[c, :, y, x], vb.at[c, :, y, x], vb.at[c, :, yp, x], y_down),
-            (kb.at[c, 0, y, xm], kb.at[c, 0, y, xm], kb.at[c, 0, y, xo], x_right),
-            (kb.at[c, 1, y, xp], kb.at[c, 1, y, xp], kb.at[c, 1, y, xo], x_left),
-            (vb.at[c, 0, ym, x], vb.at[c, 0, ym, x], vb.at[c, 0, yo, x], y_up),
-            (vb.at[c, 1, yp, x], vb.at[c, 1, yp, x], vb.at[c, 1, yo, x], y_down),
+            (vb.at[c, :, y, x], vb.at[c, :, y, x], vb.at[c, :, yo, x], y_far),
             (kb.at[c, :, y], kb.at[c, :, y], kb.at[c, :, ym], y_up),
             (kb.at[c, :, y], kb.at[c, :, y], kb.at[c, :, yp], y_down),
+            (kb.at[c, :, y], kb.at[c, :, y], kb.at[c, :, yo], y_far),
             (vb.at[c, :, :, x], vb.at[c, :, :, x], vb.at[c, :, :, xm], x_right),
             (vb.at[c, :, :, x], vb.at[c, :, :, x], vb.at[c, :, :, xp], x_left),
-            (kb.at[c, 0, ym], kb.at[c, 0, ym], kb.at[c, 0, yo], y_up),
-            (kb.at[c, 1, yp], kb.at[c, 1, yp], kb.at[c, 1, yo], y_down),
-            (vb.at[c, 0, :, xm], vb.at[c, 0, :, xm], vb.at[c, 0, :, xo], x_right),
-            (vb.at[c, 1, :, xp], vb.at[c, 1, :, xp], vb.at[c, 1, :, xo], x_left),
+            (vb.at[c, :, :, x], vb.at[c, :, :, x], vb.at[c, :, :, xo], x_far),
         )
 
     meta_routes = (
         (meta.at[zl, y, x], meta.at[zo, y, x], z_other),
         (meta.at[:, y, x], meta.at[:, y, xm], x_right),
         (meta.at[:, y, x], meta.at[:, y, xp], x_left),
-        (meta.at[0, y, xm], meta.at[0, y, xo], x_right),
-        (meta.at[1, y, xp], meta.at[1, y, xo], x_left),
+        (meta.at[:, y, x], meta.at[:, y, xo], x_far),
         (meta.at[:, y], meta.at[:, ym], y_up),
         (meta.at[:, y], meta.at[:, yp], y_down),
-        (meta.at[0, ym], meta.at[0, yo], y_up),
-        (meta.at[1, yp], meta.at[1, yo], y_down),
+        (meta.at[:, y], meta.at[:, yo], y_far),
     )
 
     def remote(c, k):
@@ -247,16 +245,26 @@
         for h in range(heads)
     ]
 
-    neighbours = (z_right, z_left, partner, z_other, x_right, x_left, y_up, y_down)
+    neighbours = (
+        z_right,
+        z_left,
+        partner,
+        z_other,
+        x_right,
+        x_left,
+        x_far,
+        y_up,
+        y_down,
+        y_far,
+    )
     barrier = pltpu.get_barrier_semaphore()
     for device in neighbours:
         pl.semaphore_signal(barrier, inc=1, device_id=device, device_id_type=MESH)
+    pl.semaphore_wait(barrier, len(neighbours))
+    for c in range(AHEAD):
+        start(c, 0, 1, 4)
     for copy in own_hidden + resident_in + weights_in + query_in:
         copy.start()
-    pl.semaphore_wait(barrier, len(neighbours))
-
-    for c in range(2):
-        start(c, 0, 1, 4)
 
     owners = [owner[i] for i in range(pages_here)]
     page_row = lax.broadcasted_iota(jnp.int32, (pages_here, lanes), 0)
@@ -265,7 +273,7 @@
         rank = jnp.int32(0)
         for j in range(i):
             rank = rank + jnp.where(owners[j] == owners[i], 1, 0).astype(jnp.int32)
-        code = owners[i] * 64 + s * 2 + rank
+        code = owners[i] * (count_full.shape[0] - pool) + s * 2 + rank
         codes = jnp.where(page_row == i, code, codes)
     meta[zl, y, x] = codes
 
@@ -301,14 +309,23 @@
     dec_sum[...] = jnp.zeros(dec_sum.shape, jnp.float32)
     dec_acc[...] = jnp.zeros(dec_acc.shape, jnp.float32)
 
-    def count_pages(page_ids):
+    tile_pages = 32
+
+    def count_pages(i, carry):
+        first = pl.multiple_of(i * tile_pages, tile_pages)
+        ids = first + lax.broadcasted_iota(jnp.int32, (tile_pages, lanes), 0)
+
         def step(j, total):
-            return total + jnp.where(page_ids == visible_pages[pl.ds(j, 1), :], 1.0, 0.0)
-
-        total = lax.fori_loop(
-            0, max_pages, step, jnp.zeros(page_ids.shape, jnp.float32), unroll=8
-        )
-        return total, jnp.where(page_ids == last_page[...], 1.0, 0.0)
+            return total + jnp.where(ids == visible_pages[pl.ds(j, 1), :], 1.0, 0.0)
+
+        count_full[pl.ds(first, tile_pages), :] = lax.fori_loop(
+            0, max_pages, step, jnp.zeros(ids.shape, jnp.float32), unroll=8
+        )
+        count_last[pl.ds(first, tile_pages), :] = jnp.where(ids == last_page[...], 1.0, 0.0)
+        return carry
+
+    lax.fori_loop(0, count_full.shape[0] // tile_pages, count_pages, 0)
+    slots = count_full.shape[0] - pool
 
     def decode_tile(keys, values, counts):
         scores = lax.dot_general(keys, dqm[...], NT, preferred_element_type=jnp.float32)
@@ -323,62 +340,50 @@
             values, weights.astype(jnp.bfloat16), TN, preferred_element_type=jnp.float32
         )
 
-    for copy in resident_in:
-        copy.wait()
-    tile_pages = 32
     token_of = lax.broadcasted_iota(jnp.int32, (PAGE, lanes), 0)
     in_last = jnp.where(token_of < last_tokens, 1.0, 0.0)
 
-    def resident_tile(i, carry):
+    def token_counts(full, last):
+        return jnp.broadcast_to(full, (PAGE, lanes)) + in_last * jnp.broadcast_to(
+            last, (PAGE, lanes)
+        )
+
+    def resident_tile(i):
         first = pl.multiple_of(i * tile_pages, tile_pages)
-        ids = first + lax.broadcasted_iota(jnp.int32, (tile_pages, lanes), 0)
-        total, last = count_pages(ids)
-        counts = [
-            jnp.broadcast_to(total[p : p + 1, :], (PAGE, lanes))
-            + in_last * jnp.broadcast_to(last[p : p + 1, :], (PAGE, lanes))
-            for p in range(tile_pages)
-        ]
+        full = count_full[pl.ds(first, tile_pages), :]
+        last = count_last[pl.ds(first, tile_pages), :]
+        counts = [token_counts(full[p : p + 1], last[p : p + 1]) for p in range(tile_pages)]
         decode_tile(
             rk[pl.ds(first, tile_pages)].reshape(tile_pages * PAGE, lanes),
             rv[pl.ds(first, tile_pages)].reshape(tile_pages * PAGE, lanes),
             jnp.concatenate(counts, axis=0),
         )
-        return carry
-
-    lax.fori_loop(0, pool // tile_pages, resident_tile, 0)
 
     def count_incoming():
-        def one(i, carry):
-            for yy in range(4):
-                code = meta[i // 4, yy, i % 4] - s * 64
-                ids = jnp.where((code >= 0) & (code < 64), code + pool, -5)
-                total, last = count_pages(ids)
-                sec = (i // 4) * 16 + yy * 4 + i % 4
-                count_full[sec] = total
-                count_last[sec] = last
-            return carry
-
-        lax.fori_loop(0, 8, one, 0)
+        slot = lax.broadcasted_iota(jnp.int32, (pages_here, lanes), 1)
+        picks = []
+        for i in range(32):
+            code = meta[i // 16, i // 4 % 4, i % 4] - s * slots
+            picks.append(jnp.where(code == slot, 1.0, 0.0).astype(jnp.bfloat16))
+        table_of = jnp.concatenate([count_full[pool:, :], count_last[pool:, :]], axis=1)
+        table_of = table_of.astype(jnp.bfloat16)
+        counts = jnp.dot(
+            jnp.concatenate(picks, axis=0)[:, :slots], table_of, preferred_element_type=jnp.float32
+        )
+        page_full[...] = counts[:, :lanes]
+        page_last[...] = counts[:, lanes:]
 
     def decode_chunk(c):
-        def one(i, carry):
-            zz, yy = i // 4, i % 4
-            counts = []
-            for xx in range(4):
-                for p in range(pages_chunk):
-                    at = pl.ds(c * pages_chunk + p, 1)
-                    counts.append(
-                        jnp.broadcast_to(count_full[i * 4 + xx, at, :], (PAGE, lanes))
-                        + in_last * jnp.broadcast_to(count_last[i * 4 + xx, at, :], (PAGE, lanes))
-                    )
-            decode_tile(
-                kb[c, zz, yy].reshape(4 * rows, lanes),
-                vb[c, zz, yy].reshape(4 * rows, lanes),
-                jnp.concatenate(counts, axis=0),
-            )
-            return carry
-
-        lax.fori_loop(0, 8, one, 0)
+        counts = []
+        for i in range(32):
+            for p in range(pages_chunk):
+                at = pl.ds(i * pages_here + c * pages_chunk + p, 1)
+                counts.append(token_counts(page_full[at, :], page_last[at, :]))
+        decode_tile(
+            kb[c].reshape(32 * rows, lanes),
+            vb[c].reshape(32 * rows, lanes),
+            jnp.concatenate(counts, axis=0),
+        )
 
     shards = hid.shape[1]
 
@@ -402,25 +407,36 @@
         vb[c, zl, y, x] = total[:, lanes:].astype(jnp.bfloat16)
 
     tile_sections = 4 * TILE_Y
-    tile_keys = tile_sections * rows
+    tile_keys = GROUP * tile_sections * rows
     tiles = 32 // tile_sections
     own_tile = s // tile_sections
 
     def attend(c, kt, hp, masked):
         first_y = kt * TILE_Y
-        keys = kb[c, first_y // 4, pl.ds(first_y % 4, TILE_Y)].reshape(tile_keys, lanes)
-        values = vb[c, first_y // 4, pl.ds(first_y % 4, TILE_Y)].reshape(tile_keys, lanes)
+        at = (pl.ds(c, GROUP), first_y // 4, pl.ds(first_y % 4, TILE_Y))
+        keys = kb[at].reshape(tile_keys, lanes)
+        values = vb[at].reshape(tile_keys, lanes)
         if masked:
             n = lax.broadcasted_iota(jnp.int32, (stretch, lanes), 1)
             query_pos = s * stretch + lax.broadcasted_iota(jnp.int32, (stretch, lanes), 0)
+        def score(i):
+            return lax.dot_general(
+                qs[hp * UNIT_HEADS + i], keys, NT, preferred_element_type=jnp.float32
+            )
+
+        following = score(0)
         for i in range(UNIT_HEADS):
             h = hp * UNIT_HEADS + i
-            scores = lax.dot_general(qs[h], keys, NT, preferred_element_type=jnp.float32)
+            scores = following
+            if i + 1 < UNIT_HEADS:
+                following = score(i + 1)
             pieces = [scores[:, j * lanes : (j + 1) * lanes] for j in range(tile_keys // lanes)]
             if masked:
                 for j in range(len(pieces)):
                     at = j * lanes + n
-                    key_pos = (kt * tile_sections + at // rows) * stretch + c * rows + at % rows
+                    part, rest = at // (tile_sections * rows), at % (tile_sections * rows)
+                    key_pos = (kt * tile_sections + rest // rows) * stretch
+                    key_pos = key_pos + (c + part) * rows + rest % rows
                     pieces[j] = jnp.where(key_pos <= query_pos, pieces[j], NEG)
             top = functools.reduce(jnp.maximum, pieces)
             old = row_max[h]
@@ -436,125 +452,108 @@
     units = tiles * head_units
     segments = 4
 
+    def live(c):
+        return (c >= 0) & (c < chunks)
+
     def first_hop(c):
         await_arrival(c, 0, 1)
         start(c, 2, 3, 5, 6)
 
-        @pl.when(c + 2 < chunks)
+        @pl.when(c + AHEAD < chunks)
         def _():
-            start(c + 2, 0, 1, 4)
+            start(c + AHEAD, 0, 1, 4)
 
     def second_hop(c):
         await_arrival(c, 2, 3)
         start(c, 7)
 
-    for copy in own_hidden + weights_in + query_in:
+    def project_and_pair(c):
+        await_arrival(c, 4, 5, 6, 7)
+        project(c)
+        start(c, 8, 9)
+
+    def first_stage(c):
+        await_arrival(c, 8, 9)
+        start(c, 10, 11, 12, 13, 14, 15)
+
+        @pl.when(c == 0)
+        def _():
+            meta_await(0)
+            meta_start(1, 2, 3)
+
+    def second_stage(c):
+        await_arrival(c, 10, 11, 12, 13, 14, 15)
+        start(c, 16, 17, 18, 19, 20, 21)
+
+        @pl.when(c == 0)
+        def _():
+            meta_await(1, 2, 3)
+            meta_start(4, 5, 6)
+
+    def gathered(c):
+        await_arrival(c, 16, 17, 18, 19, 20, 21)
+
+        @pl.when(c == 0)
+        def _():
+            meta_await(4, 5, 6)
+            count_incoming()
+
+    plan = (
+        (0, 2, project_and_pair),
+        (0, LAG, gathered),
+        (0, 0, first_hop),
+        (0, 3, first_stage),
+        (2, 1, second_hop),
+        (2, 4, second_stage),
+    )
+
+    for copy in own_hidden + weights_in + query_in + resident_in:
         copy.wait()
-    first_hop(0)
-    second_hop(0)
-
-    def live(c):
-        return (c >= 0) & (c < chunks)
 
     def segment(g, carry):
         period, seg = g // segments, g % segments
-        ready = period - 2
-
-        @pl.when((seg == 0) & live(ready))
+        ready = period - LAG
+
+        for at, lag, handler in plan:
+
+            @pl.when((seg == at) & live(period - lag))
+            def _(handler=handler, lag=lag):
+                handler(period - lag)
+
+        @pl.when(g < pool // tile_pages)
         def _():
-            await_arrival(ready, 22, 23, 24, 25)
-
-            @pl.when(ready == 0)
-            def _():
-                meta_await(7, 8)
-
-        @pl.when((seg == 1) & live(period))
+            resident_tile(g)
+
+        beat = ready - (GROUP - 1)
+
+        @pl.when((beat >= 0) & (beat < chunks))
         def _():
-            c = period
-            await_arrival(c, 4, 5, 6, 7)
-            project(c)
-            start(c, 8, 9)
-
-        @pl.when((seg == 1) & live(period - 1))
-        def _():
-            c = period - 1
-            await_arrival(c, 14, 15, 16, 17)
-            start(c, 18, 19, 20, 21)
-
-            @pl.when(c == 0)
-            def _():
-                meta_await(3, 4)
-                meta_start(5, 6)
-
-        @pl.when((seg == 2) & live(period + 1))
-        def _():
-            first_hop(period + 1)
-
-        @pl.when((seg == 2) & live(period))
-        def _():
-            c = period
-            await_arrival(c, 8, 9)
-            start(c, 10, 11, 12, 13)
-
-            @pl.when(c == 0)
-            def _():
-                meta_await(0)
-                meta_start(1, 2)
-
-        @pl.when((seg == 3) & live(period - 1))
-        def _():
-            c = period - 1
-            await_arrival(c, 18, 19, 20, 21)
-            start(c, 22, 23, 24, 25)
-
-            @pl.when(c == 0)
-            def _():
-                meta_await(5, 6)
-                meta_start(7, 8)
-
-        @pl.when((seg == 3) & live(period))
-        def _():
-            c = period
-            await_arrival(c, 10, 11, 12, 13)
-            start(c, 14, 15, 16, 17)
-
-            @pl.when(c == 0)
-            def _():
-                meta_await(1, 2)
-                meta_start(3, 4)
-
-        @pl.when((seg == 3) & live(period + 1))
-        def _():
-            second_hop(period + 1)
-
-        @pl.when(live(ready))
-        def _():
+            group = beat // GROUP * GROUP
+            stage = beat % GROUP * segments + seg
+            stages = GROUP * segments
+
             def one(u, inner):
                 kt, hp = u // head_units, u % head_units
 
                 @pl.when(kt < own_tile)
                 def _():
-                    attend(ready, kt, hp, False)
+                    attend(group, kt, hp, False)
 
                 @pl.when(kt == own_tile)
                 def _():
-                    attend(ready, kt, hp, True)
+                    attend(group, kt, hp, True)
 
                 return inner
 
-            lax.fori_loop(seg * units // segments, (seg + 1) * units // segments, one, 0)
+            lax.fori_loop(stage * units // stages, (stage + 1) * units // stages, one, 0)
 
         @pl.when((seg == segments - 1) & live(ready))
         def _():
-            @pl.when(ready == 0)
-            def _():
-                count_incoming()
-
             decode_chunk(ready)
 
         return carry
 
-    lax.fori_loop(0, (chunks + 2) * segments, segment, 0)
+    lax.fori_loop(0, (chunks + LAG + GROUP - 1) * segments, segment, 0)
 
     for h in range(heads):
         total = jnp.sum(row_sum[h], axis=1, keepdims=True)
@@ -639,8 +638,10 @@
             pltpu.VMEM((heads, stretch, HD), f32),
             pltpu.VMEM((block_table.shape[1], HD), i32),
             pltpu.VMEM((1, HD), i32),
-            pltpu.VMEM((32, stretch // PAGE, HD), f32),
-            pltpu.VMEM((32, stretch // PAGE, HD), f32),
+            pltpu.VMEM((pool + 64, HD), f32),
+            pltpu.VMEM((pool + 64, HD), f32),
+            pltpu.VMEM((32 * stretch // PAGE, HD), f32),
+            pltpu.VMEM((32 * stretch // PAGE, HD), f32),
             pltpu.VMEM((1, HD), f32),
             pltpu.VMEM((1, HD), f32),
             pltpu.VMEM((HD, HD), f32),

time: 119 us -> 92.3 us (0.78)
  Pallas kernels: 115 us -> 88.2 us
    pallas_call x1, Pallas kernels: 115 us -> 88.2 us  [per_device(): pl.pallas_call(kernel, out_shape=(jax.ShapeDtypeStruct(prefill_query.shap...]
where the time goes in v2:
time: 92.3 us; the launch traced here: 92.1 us
  Pallas kernels  88.2 us (96%)
  local copies, waits for them, and re-layouts  3.24 us (4%)
    pallas_call x1, Pallas kernels, per_device(): pl.pallas_call(kernel, out_shape=(jax.ShapeDtypeStruct(prefill_query.shap...  88.2 us
    unnamed x2, local copies, waits for them, and re-layouts  3.24 us

profile of v2, /device:TPU:32, one launch (start us, length us, event | category | flops | bytes accessed | tf_op | source)
XLA Modules:
  0.0 92.1 jit_solution(13880961520815602884)
XLA Ops:
  0.6 88.2 %attention_layer.1 = (bf16[256,1024]{1,0:T(8,128)(2,1)}, bf16[16,1024]{1,0:T(8,128)(2,1)}) custom-call(bf16[256,1024]{1,0:T(8,128)(2,1)} %hidden.1, f32[1,8192]{1,0:T(1,128)} %bitcast.1, bf16[8192,128]{1,0:T(8,128)(2,1)} %key_weight.1, bf16[8192,128]{1,0:T(8,128)(2,1)} %value_weight.1, bf16[256,1024]{1,0:T(8,128)(2,1)} %query.1, ...), custom_call_target="tpu_custom_call" | custom-call | tf_op jit(solution)/shard_map/attention_layer/pallas_call | solution.py:600
  88.8 1.9 %copy.19 = bf16[256,1024]{1,0:T(8,128)(2,1)} copy(bf16[256,1024]{1,0:T(8,128)(2,1)} %get-tuple-element.4) | data formatting | bytes 1048576
  90.7 1.4 %copy.20 = bf16[16,1024]{1,0:T(8,128)(2,1)} copy(bf16[16,1024]{1,0:T(8,128)(2,1)} %get-tuple-element.5) | data formatting | bytes 65536

commit v3 on v2

--- a/solution.py
+++ b/solution.py
@@ -18,11 +18,12 @@
 NEG = -1e30
 CHUNKS = 8
 TILE_Y = 4
-UNIT_HEADS = 4
+UNIT_HEADS = 8
 GROUP = 2
 LAG = 6
 AHEAD = 2
-N_COPIES = 22
+GROUPS = ((0, 1), (2, 3), (4, 5, 6, 7), (8, 9), (10, 11, 12, 13, 14, 15), (16, 17, 18, 19, 20, 21))
+GROUP_OF = tuple(g for g, ks in enumerate(GROUPS) for _ in ks)
 N_META = 7
 POW = math.log2(math.e) / math.sqrt(HD)
 
@@ -81,8 +82,8 @@
     last_page,
     count_full,
     count_last,
-    page_full,
-    page_last,
+    slot_page,
+    slot_index,
     dec_max,
     dec_sum,
     dec_acc,
@@ -112,7 +113,6 @@
     t_r, t_l, t_o = ((zh + 1) % 4) * 2 + core, ((zh + 3) % 4) * 2 + core, ((zh + 2) % 4) * 2 + core
     other = 1 - core
     t_p = zh * 2 + other
-    p_r, p_l, p_o = ((zh + 1) % 4) * 2 + other, ((zh + 3) % 4) * 2 + other, ((zh + 2) % 4) * 2 + other
     xp, xm, xo = (x + 1) % 4, (x + 3) % 4, (x + 2) % 4
     yp, ym, yo = (y + 1) % 4, (y + 3) % 4, (y + 2) % 4
     zo = 1 - zl
@@ -130,28 +130,28 @@
         top, bottom = pl.ds(0, half_rows), pl.ds(half_rows, half_rows)
         mine = hidden.at[pl.ds(pl.multiple_of(c * rows, rows), rows), :]
         return (
-            (mine, hid.at[c, t], hid.at[c, t_l], z_right),
-            (mine, hid.at[c, t], hid.at[c, t_r], z_left),
-            (hid.at[c, t_l, top], hid.at[c, t_l, top], hid.at[c, t_o, top], z_right),
-            (hid.at[c, t_r, bottom], hid.at[c, t_r, bottom], hid.at[c, t_o, bottom], z_left),
-            (mine, hid.at[c, t], hid.at[c, t_p], partner),
-            (hid.at[c, t_l], hid.at[c, t_l], hid.at[c, p_l], partner),
-            (hid.at[c, t_r], hid.at[c, t_r], hid.at[c, p_r], partner),
-            (hid.at[c, t_o], hid.at[c, t_o], hid.at[c, p_o], partner),
-            (kb.at[c, zl, y, x], kb.at[c, zl, y, x], kb.at[c, zo, y, x], z_other),
-            (vb.at[c, zl, y, x], vb.at[c, zl, y, x], vb.at[c, zo, y, x], z_other),
-            (kb.at[c, :, y, x], kb.at[c, :, y, x], kb.at[c, :, y, xm], x_right),
-            (kb.at[c, :, y, x], kb.at[c, :, y, x], kb.at[c, :, y, xp], x_left),
-            (kb.at[c, :, y, x], kb.at[c, :, y, x], kb.at[c, :, y, xo], x_far),
-            (vb.at[c, :, y, x], vb.at[c, :, y, x], vb.at[c, :, ym, x], y_up),
-            (vb.at[c, :, y, x], vb.at[c, :, y, x], vb.at[c, :, yp, x], y_down),
-            (vb.at[c, :, y, x], vb.at[c, :, y, x], vb.at[c, :, yo, x], y_far),
-            (kb.at[c, :, y], kb.at[c, :, y], kb.at[c, :, ym], y_up),
-            (kb.at[c, :, y], kb.at[c, :, y], kb.at[c, :, yp], y_down),
-            (kb.at[c, :, y], kb.at[c, :, y], kb.at[c, :, yo], y_far),
-            (vb.at[c, :, :, x], vb.at[c, :, :, x], vb.at[c, :, :, xm], x_right),
-            (vb.at[c, :, :, x], vb.at[c, :, :, x], vb.at[c, :, :, xp], x_left),
-            (vb.at[c, :, :, x], vb.at[c, :, :, x], vb.at[c, :, :, xo], x_far),
+            (mine, hid.at[c, t], z_right),
+            (mine, hid.at[c, t], z_left),
+            (hid.at[c, t_l, top], hid.at[c, t_l, top], z_right),
+            (hid.at[c, t_r, bottom], hid.at[c, t_r, bottom], z_left),
+            (mine, hid.at[c, t], partner),
+            (hid.at[c, t_l], hid.at[c, t_l], partner),
+            (hid.at[c, t_r], hid.at[c, t_r], partner),
+            (hid.at[c, t_o], hid.at[c, t_o], partner),
+            (kb.at[c, zl, y, x], kb.at[c, zl, y, x], z_other),
+            (vb.at[c, zl, y, x], vb.at[c, zl, y, x], z_other),
+            (kb.at[c, :, y, x], kb.at[c, :, y, x], x_right),
+            (kb.at[c, :, y, x], kb.at[c, :, y, x], x_left),
+            (kb.at[c, :, y, x], kb.at[c, :, y, x], x_far),
+            (vb.at[c, :, y, x], vb.at[c, :, y, x], y_up),
+            (vb.at[c, :, y, x], vb.at[c, :, y, x], y_down),
+            (vb.at[c, :, y, x], vb.at[c, :, y, x], y_far),
+            (kb.at[c, :, y], kb.at[c, :, y], y_up),
+            (kb.at[c, :, y], kb.at[c, :, y], y_down),
+            (kb.at[c, :, y], kb.at[c, :, y], y_far),
+            (vb.at[c, :, :, x], vb.at[c, :, :, x], x_right),
+            (vb.at[c, :, :, x], vb.at[c, :, :, x], x_left),
+            (vb.at[c, :, :, x], vb.at[c, :, :, x], x_far),
         )
 
     meta_routes = (
@@ -165,24 +165,31 @@
     )
 
     def remote(c, k):
-        source, target, _, device = routes(c)[k]
+        source, target, device = routes(c)[k]
         return pltpu.make_async_remote_copy(
             src_ref=source,
             dst_ref=target,
-            send_sem=send_sem.at[c, k],
-            recv_sem=recv_sem.at[c, k],
+            send_sem=send_sem.at[c, GROUP_OF[k]],
+            recv_sem=recv_sem.at[c, GROUP_OF[k]],
             device_id=device,
             device_id_type=MESH,
         )
 
-    def arrival(c, k):
-        _, _, landing, device = routes(c)[k]
+    def whole(c, g):
+        view = (
+            hid.at[c, pl.ds(0, 2)],
+            hid.at[c, 0],
+            hid.at[c, pl.ds(0, 4)],
+            kb.at[c, 0, 0, pl.ds(0, 2)],
+            kb.at[c, 0, pl.ds(0, 3)],
+            hid.at[c, pl.ds(0, 6)],
+        )[g]
         return pltpu.make_async_remote_copy(
-            src_ref=landing,
-            dst_ref=landing,
-            send_sem=send_sem.at[c, k],
-            recv_sem=recv_sem.at[c, k],
-            device_id=device,
+            src_ref=view,
+            dst_ref=view,
+            send_sem=send_sem.at[c, g],
+            recv_sem=recv_sem.at[c, g],
+            device_id=partner,
             device_id_type=MESH,
         )
 
@@ -191,8 +198,9 @@
             remote(c, k).start()
 
     def await_arrival(c, *ks):
-        for k in ks:
-            arrival(c, k).wait_recv()
+        g = GROUP_OF[ks[0]]
+        assert GROUPS[g] == ks
+        whole(c, g).wait_recv()
 
     def meta_copy(k):
         source, _, device = meta_routes[k]
@@ -324,7 +332,6 @@
         count_last[pl.ds(first, tile_pages), :] = jnp.where(ids == last_page[...], 1.0, 0.0)
         return carry
 
-    lax.fori_loop(0, count_full.shape[0] // tile_pages, count_pages, 0)
     slots = count_full.shape[0] - pool
 
     def decode_tile(keys, values, counts):
@@ -359,29 +366,41 @@
             jnp.concatenate(counts, axis=0),
         )
 
-    def count_incoming():
-        slot = lax.broadcasted_iota(jnp.int32, (pages_here, lanes), 1)
-        picks = []
+    page_copy = pltpu.make_async_copy(slot_page, slot_index, local_sem.at[chunks + 4 + heads])
+
+    def find_pages():
+        lane = lax.broadcasted_iota(jnp.int32, (pages_here, lanes), 1)
+        found = jnp.zeros((pages_here, lanes), jnp.int32)
         for i in range(32):
-            code = meta[i // 16, i // 4 % 4, i % 4] - s * slots
-            picks.append(jnp.where(code == slot, 1.0, 0.0).astype(jnp.bfloat16))
-        table_of = jnp.concatenate([count_full[pool:, :], count_last[pool:, :]], axis=1)
-        table_of = table_of.astype(jnp.bfloat16)
-        counts = jnp.dot(
-            jnp.concatenate(picks, axis=0)[:, :slots], table_of, preferred_element_type=jnp.float32
-        )
-        page_full[...] = counts[:, :lanes]
-        page_last[...] = counts[:, lanes:]
-
-    def decode_chunk(c):
-        counts = []
-        for i in range(32):
-            for p in range(pages_chunk):
-                at = pl.ds(i * pages_here + c * pages_chunk + p, 1)
-                counts.append(token_counts(page_full[at, :], page_last[at, :]))
+            here = (meta[i // 16, i // 4 % 4, i % 4] == s * slots + lane) & (lane // 2 == i)
+            found = found + jnp.where(here, page_row, 0)
+        page = jnp.minimum(jnp.sum(found, axis=0, keepdims=True), pages_here - 1)
+        slot_page[0:1, :] = page // pages_chunk
+        slot_page[1:2, :] = page % pages_chunk
+
+    def decode_incoming():
+        page_copy.wait()
+
+        def fetch(k, carry):
+            sec = k // 2
+            chunk, page = slot_index[0, k], slot_index[1, k]
+            keys = kb[chunk, sec // 16, sec // 4 % 4, sec % 4]
+            values = vb[chunk, sec // 16, sec // 4 % 4, sec % 4]
+            first, second = keys[:PAGE], values[:PAGE]
+            for p in range(1, pages_chunk):
+                part = slice(p * PAGE, (p + 1) * PAGE)
+                first = jnp.where(page == p, keys[part], first)
+                second = jnp.where(page == p, values[part], second)
+            rk[k] = first
+            rv[k] = second
+            return carry
+
+        lax.fori_loop(0, slots, fetch, 0, unroll=4)
+        full, last = count_full[pool:, :], count_last[pool:, :]
+        counts = [token_counts(full[p : p + 1], last[p : p + 1]) for p in range(slots)]
         decode_tile(
-            kb[c].reshape(32 * rows, lanes),
-            vb[c].reshape(32 * rows, lanes),
+            rk[:slots].reshape(slots * PAGE, lanes),
+            rv[:slots].reshape(slots * PAGE, lanes),
             jnp.concatenate(counts, axis=0),
         )
 
@@ -417,7 +436,7 @@
         keys = kb[at].reshape(tile_keys, lanes)
         values = vb[at].reshape(tile_keys, lanes)
         if masked:
-            n = lax.broadcasted_iota(jnp.int32, (stretch, lanes), 1)
+            n = lax.broadcasted_iota(jnp.int32, (1, lanes), 1)
             query_pos = s * stretch + lax.broadcasted_iota(jnp.int32, (stretch, lanes), 0)
         def score(i):
             return lax.dot_general(
@@ -496,7 +515,7 @@
         @pl.when(c == 0)
         def _():
             meta_await(4, 5, 6)
-            count_incoming()
+            find_pages()
 
     plan = (
         (0, 2, project_and_pair),
@@ -520,9 +539,17 @@
             def _(handler=handler, lag=lag):
                 handler(period - lag)
 
-        @pl.when(g < pool // tile_pages)
+        @pl.when(g == (LAG + 1) * segments)
         def _():
-            resident_tile(g)
+            page_copy.start()
+
+        @pl.when(g == 1)
+        def _():
+            lax.fori_loop(0, count_full.shape[0] // tile_pages, count_pages, 0)
+
+        @pl.when((g >= 4) & (g < 4 + pool // tile_pages))
+        def _():
+            resident_tile(g - 4)
 
         beat = ready - (GROUP - 1)
 
@@ -547,14 +574,11 @@
 
             lax.fori_loop(stage * units // stages, (stage + 1) * units // stages, one, 0)
 
-        @pl.when((seg == segments - 1) & live(ready))
-        def _():
-            decode_chunk(ready)
-
         return carry
 
     lax.fori_loop(0, (chunks + LAG + GROUP - 1) * segments, segment, 0)
 
+    decode_incoming()
     for h in range(heads):
         total = jnp.sum(row_sum[h], axis=1, keepdims=True)
         out[:, h * lanes : (h + 1) * lanes] = (acc[h] / total).astype(out.dtype)
@@ -565,8 +589,8 @@
         ].astype(decode_out.dtype)
 
     def drain(c, carry):
-        for k in range(N_COPIES):
-            remote(c, k).wait_send()
+        for g in range(len(GROUPS)):
+            whole(c, g).wait_send()
         return carry
 
     lax.fori_loop(0, chunks, drain, 0)
@@ -640,14 +664,14 @@
             pltpu.VMEM((1, HD), i32),
             pltpu.VMEM((pool + 64, HD), f32),
             pltpu.VMEM((pool + 64, HD), f32),
-            pltpu.VMEM((32 * stretch // PAGE, HD), f32),
-            pltpu.VMEM((32 * stretch // PAGE, HD), f32),
+            pltpu.VMEM((2, HD), i32),
+            pltpu.SMEM((2, HD), i32),
             pltpu.VMEM((1, HD), f32),
             pltpu.VMEM((1, HD), f32),
             pltpu.VMEM((HD, HD), f32),
-            pltpu.SemaphoreType.DMA((CHUNKS + 4 + heads,)),
-            pltpu.SemaphoreType.DMA((CHUNKS, N_COPIES)),
-            pltpu.SemaphoreType.DMA((CHUNKS, N_COPIES)),
+            pltpu.SemaphoreType.DMA((CHUNKS + 5 + heads,)),
+            pltpu.SemaphoreType.DMA((CHUNKS, len(GROUPS))),
+            pltpu.SemaphoreType.DMA((CHUNKS, len(GROUPS))),
             pltpu.SemaphoreType.DMA((N_META,)),
             pltpu.SemaphoreType.DMA((N_META,)),
         ],

time: 92.3 us -> 86 us (0.932)
  Pallas kernels: 88.2 us -> 81.9 us
    pallas_call x1, Pallas kernels: 88.2 us -> 81.9 us  [per_device(): pl.pallas_call(kernel, out_shape=(jax.ShapeDtypeStruct(prefill_query.shap...]
where the time goes in v3:
time: 86 us; the launch traced here: 85.8 us
  Pallas kernels  81.9 us (95%)
  local copies, waits for them, and re-layouts  3.24 us (4%)
    pallas_call x1, Pallas kernels, per_device(): pl.pallas_call(kernel, out_shape=(jax.ShapeDtypeStruct(prefill_query.shap...  81.9 us
    unnamed x2, local copies, waits for them, and re-layouts  3.24 us

profile of v3, /device:TPU:32, one launch (start us, length us, event | category | flops | bytes accessed | tf_op | source)
XLA Modules:
  0.0 85.8 jit_solution(4414245089342795438)
XLA Ops:
  0.6 81.9 %attention_layer.1 = (bf16[256,1024]{1,0:T(8,128)(2,1)}, bf16[16,1024]{1,0:T(8,128)(2,1)}) custom-call(bf16[256,1024]{1,0:T(8,128)(2,1)} %hidden.1, f32[1,8192]{1,0:T(1,128)} %bitcast.1, bf16[8192,128]{1,0:T(8,128)(2,1)} %key_weight.1, bf16[8192,128]{1,0:T(8,128)(2,1)} %value_weight.1, bf16[256,1024]{1,0:T(8,128)(2,1)} %query.1, ...), custom_call_target="tpu_custom_call" | custom-call | tf_op jit(solution)/shard_map/attention_layer/pallas_call | solution.py:624
  82.6 1.9 %copy.19 = bf16[256,1024]{1,0:T(8,128)(2,1)} copy(bf16[256,1024]{1,0:T(8,128)(2,1)} %get-tuple-element.4) | data formatting | bytes 1048576
  84.5 1.4 %copy.20 = bf16[16,1024]{1,0:T(8,128)(2,1)} copy(bf16[16,1024]{1,0:T(8,128)(2,1)} %get-tuple-element.5) | data formatting | bytes 65536

commit v4 on v3

--- a/solution.py
+++ b/solution.py
@@ -598,6 +598,11 @@
         meta_copy(k).wait_send()
 
 
+def store(prefill, decode, prefill_out, decode_out):
+    prefill_out[...] = prefill[...]
+    decode_out[...] = decode[...]
+
+
 def per_device(
     prefill_hidden,
     norm_gain,
@@ -621,7 +626,7 @@
     vmem = pl.BlockSpec(memory_space=pltpu.VMEM)
     smem = pl.BlockSpec(memory_space=pltpu.SMEM)
     f32, bf16, i32 = jnp.float32, jnp.bfloat16, jnp.int32
-    return pl.pallas_call(
+    attended = pl.pallas_call(
         kernel,
         out_shape=(
             jax.ShapeDtypeStruct(prefill_query.shape, bf16),
@@ -693,6 +698,13 @@
         context_len,
         *tables,
     )
+    return pl.pallas_call(
+        store,
+        out_shape=tuple(jax.ShapeDtypeStruct(each.shape, each.dtype) for each in attended),
+        in_specs=[vmem, vmem],
+        out_specs=(vmem, vmem),
+        name="store",
+    )(*attended)
 
 
 def solution(mesh):

time: 86 us -> 84.6 us (0.984)
  local copies, waits for them, and re-layouts: 3.24 us -> 0 us
  Pallas kernels: 81.9 us -> 83.8 us
    unnamed x2 -> x0, local copies, waits for them, and re-layouts: 3.24 us -> none
    pallas_call x0 -> x1, Pallas kernels: none -> 1.87 us  [per_device(): pl.pallas_call(store, out_shape=tuple((jax.ShapeDtypeStruct(each.shape, e...]
where the time goes in v4:
time: 84.6 us; the launch traced here: 84.5 us
  Pallas kernels  83.8 us (99%)
    pallas_call x1, Pallas kernels, per_device(): pl.pallas_call(kernel, out_shape=(jax.ShapeDtypeStruct(prefill_query.shap...  81.9 us
    pallas_call x1, Pallas kernels, per_device(): pl.pallas_call(store, out_shape=tuple((jax.ShapeDtypeStruct(each.shape, e...  1.87 us

profile of v4, /device:TPU:32, one launch (start us, length us, event | category | flops | bytes accessed | tf_op | source)
XLA Modules:
  0.0 84.5 jit_solution(3043120241788516840)
XLA Ops:
  0.6 81.9 %attention_layer.1 = (bf16[256,1024]{1,0:T(8,128)(2,1)}, bf16[16,1024]{1,0:T(8,128)(2,1)}) custom-call(bf16[256,1024]{1,0:T(8,128)(2,1)} %hidden.1, f32[1,8192]{1,0:T(1,128)} %bitcast.1, bf16[8192,128]{1,0:T(8,128)(2,1)} %key_weight.1, bf16[8192,128]{1,0:T(8,128)(2,1)} %value_weight.1, bf16[256,1024]{1,0:T(8,128)(2,1)} %query.1, ...), custom_call_target="tpu_custom_call" | custom-call | tf_op jit(solution)/shard_map/attention_layer/pallas_call | solution.py:629
  82.6 1.9 %store.1 = (bf16[256,1024]{1,0:T(8,128)(2,1)}, bf16[16,1024]{1,0:T(8,128)(2,1)}) custom-call(bf16[256,1024]{1,0:T(8,128)(2,1)} %get-tuple-element.4.prefill, bf16[16,1024]{1,0:T(8,128)(2,1)} %get-tuple-element.5.decode), custom_call_target="tpu_custom_call" | custom-call | tf_op jit(solution)/shard_map/store/pallas_call | solution.py:701
